TPU v7x, 32 devices: a whole 2x2x4 slice. The times are simulated.
32 devices in a mesh: row: 8 (over z, x), col: 4 (over y, core).
Axes of the slice: x: 2, y: 2, z: 4, core: 2. Of those that a mesh axis runs over, the one named last changes fastest.
Arguments:
- alignment: bfloat16 [256, 192, 256], P('row', 'col'), may hold values from -8 to 8
- alignment_mask: int32 [256, 192], P('row', 'col'), may hold values from 0 to 1, as said below
- residue_mask: int32 [192], replicated, may hold values from 0 to 1, as said below
- pair_features: bfloat16 [192, 192, 128], P('row', 'col'), may hold values from -6 to 6
- outer_product_left: bfloat16 [256, 32], replicated, may hold values from -0.375 to 0.375
- outer_product_right: bfloat16 [256, 32], replicated, may hold values from -0.375 to 0.375
- outer_proj: bfloat16 [1024, 128], replicated, may hold values from -0.1875 to 0.1875
- triangle_proj: bfloat16 [128, 512], replicated, may hold values from -0.5 to 0.5
- triangle_gate: bfloat16 [128, 128], replicated, may hold values from -0.5 to 0.5
- triangle_out: bfloat16 [128, 128], replicated, may hold values from -0.5 to 0.5
- transition_in: bfloat16 [128, 512], replicated, may hold values from -0.5 to 0.5
- transition_out: bfloat16 [512, 128], replicated, may hold values from -0.25 to 0.25
Outputs:
- pair_out: bfloat16 [192, 192, 128], P('row', 'col')
Inputs may be any that keep to these rules, and one draw needn't show every extreme that they name: `residue_mask`: masked residues scattered anywhere; at least one residue is masked and at least one takes part. `alignment_mask`: 0 wherever residue_mask is 0.
All inputs are finite; a program needn't handle non-finite values.
Results may differ from a plain program's by a relative error of at most 0.014.
Values may be sent and summed in bfloat16 or wider, within the bound.
No kernel may reach another device: no remote copies, remote signals or barrier semaphores. Data moves between devices by JAX's collectives and lax.ppermute only.
A program may use at most 64 MiB of HBM per device.

v0:
```python
import jax
import jax.numpy as jnp
from jax import lax
from jax.sharding import PartitionSpec as P

epsilon = 1e-05


def normalize(values):
    mean_value = jnp.mean(values, axis=-1, keepdims=True)
    centered = values - mean_value
    variance = jnp.mean(centered * centered, axis=-1, keepdims=True)
    return centered * lax.rsqrt(variance + epsilon)


def shards(
    alignment,
    alignment_mask,
    residue_mask,
    pair_features,
    outer_product_left,
    outer_product_right,
    outer_proj,
    triangle_proj,
    triangle_gate,
    triangle_out,
    transition_in,
    transition_out,
):
    block_rows, block_cols, channels = pair_features.shape
    inner = triangle_out.shape[0]
    narrow = outer_product_left.shape[1]
    mask_float = alignment_mask.astype(jnp.float32)
    normed = normalize(alignment.astype(jnp.float32)).astype(jnp.bfloat16)
    left_side = (
        jnp.dot(normed, outer_product_left, preferred_element_type=jnp.float32)
        * mask_float[..., None]
    ).astype(jnp.bfloat16)
    right_side = (
        jnp.dot(normed, outer_product_right, preferred_element_type=jnp.float32)
        * mask_float[..., None]
    ).astype(jnp.bfloat16)
    mask_wire = alignment_mask.astype(jnp.bfloat16)
    right_all, right_mask = (
        lax.all_gather(right_side, "row", axis=0, tiled=True),
        lax.all_gather(mask_wire, "row", axis=0, tiled=True),
    )
    left_rows, left_row_mask = (
        lax.all_gather(left_side, "col", axis=1, tiled=True),
        lax.all_gather(mask_wire, "col", axis=1, tiled=True),
    )
    left_all, left_mask = (
        lax.all_to_all(left_rows, "row", split_axis=1, concat_axis=0, tiled=True),
        lax.all_to_all(left_row_mask, "row", split_axis=1, concat_axis=0, tiled=True),
    )
    sequences = left_all.shape[0]
    contract = (((0,), (0,)), ((), ()))
    outer = lax.dot_general(
        left_all.reshape(sequences, block_rows * narrow),
        right_all.reshape(sequences, block_cols * narrow),
        contract,
        preferred_element_type=jnp.float32,
    )
    outer = (
        outer.reshape(block_rows, narrow, block_cols, narrow)
        .transpose(0, 2, 1, 3)
        .astype(jnp.bfloat16)
    )
    outer = outer.reshape(block_rows, block_cols, narrow * narrow)
    projected = jnp.dot(outer, outer_proj, preferred_element_type=jnp.float32)
    counts = lax.dot_general(left_mask, right_mask, contract, preferred_element_type=jnp.float32)
    first = (
        pair_features.astype(jnp.float32) + projected / jnp.maximum(counts, 1.0)[..., None]
    ).astype(jnp.bfloat16)
    normed_pair = normalize(first.astype(jnp.float32)).astype(jnp.bfloat16)
    projections = jnp.dot(normed_pair, triangle_proj, preferred_element_type=jnp.float32)
    row_mask = lax.dynamic_slice_in_dim(
        residue_mask, lax.axis_index("row") * block_rows, block_rows
    ).astype(jnp.float32)
    col_mask = lax.dynamic_slice_in_dim(
        residue_mask, lax.axis_index("col") * block_cols, block_cols
    ).astype(jnp.float32)
    pair_mask = (row_mask[:, None] * col_mask[None, :])[..., None]
    left_tri = (
        jax.nn.sigmoid(projections[..., :inner]) * projections[..., inner : 2 * inner] * pair_mask
    ).astype(jnp.bfloat16)
    right_tri = (
        jax.nn.sigmoid(projections[..., 2 * inner : 3 * inner])
        * projections[..., 3 * inner :]
        * pair_mask
    ).astype(jnp.bfloat16)
    right_cols = lax.all_gather(right_tri, "row", axis=0, tiled=True)
    right_rows = lax.all_to_all(right_cols, "col", split_axis=0, concat_axis=1, tiled=True)
    summed = jnp.einsum(
        "ikc,jkc->ijc",
        lax.all_gather(left_tri, "col", axis=1, tiled=True),
        right_rows,
        preferred_element_type=jnp.float32,
    )
    normed_sum = normalize(summed).astype(jnp.bfloat16)
    update = jax.nn.sigmoid(
        jnp.dot(normed_pair, triangle_gate, preferred_element_type=jnp.float32)
    ) * jnp.dot(normed_sum, triangle_out, preferred_element_type=jnp.float32)
    second = (first.astype(jnp.float32) + update).astype(jnp.bfloat16)
    normed_second = normalize(second.astype(jnp.float32)).astype(jnp.bfloat16)
    hidden_units = jnp.maximum(
        jnp.dot(normed_second, transition_in, preferred_element_type=jnp.float32), 0.0
    ).astype(jnp.bfloat16)
    return (
        second.astype(jnp.float32)
        + jnp.dot(hidden_units, transition_out, preferred_element_type=jnp.float32)
    ).astype(jnp.bfloat16)


def solution(mesh):
    placed = (
        P("row", "col", None),
        P("row", "col"),
        P(),
        P("row", "col", None),
        P(),
        P(),
        P(),
        P(),
        P(),
        P(),
        P(),
        P(),
    )
    return jax.shard_map(
        shards, mesh=mesh, in_specs=placed, out_specs=P("row", "col", None), check_vma=False
    )
```

profile of v0, /device:TPU:0, one launch (start us, length us, event | category | flops | bytes accessed | tf_op | source)
XLA Modules:
  0.0 276.2 jit_solution(16021958013082864905)
XLA Ops:
  7.4 6.2 %all-gather = bf16[4,48,32]{1,2,0:T(8,128)(2,1)S(1)} all-gather(bf16[1,48,32]{1,2,0:T(8,128)(2,1)S(1)} %bitcast.93), channel_id=1, replica_groups=mesh['row'=8,'col'=4] {'col'}, dimensions={0}, use_global_device_ids=true | all-gather | bytes 15360 | tf_op jit(solution)/shard_map/all_gather | solution.py:50
  14.5 6.2 %all-to-all-start.1 = ((bf16[8,2,384]{2,1,0:T(2,128)(2,1)}), bf16[8,2,384]{2,1,0:T(2,128)(2,1)S(1)}, u32[]{:S(2)}, u32[]{:S(2)}) async-start(bf16[8,2,384]{2,1,0:T(2,128)(2,1)} %reshape.110), calls=%async_computation.1 | async-start | bytes 24576 | tf_op jit(solution)/shard_map/all_to_all | solution.py:54
  20.8 1.4 convert_reduce_fusion
  24.1 13.4 %all_gather.18 = bf16[32,192,32]{2,0,1:T(8,128)(2,1)} all-gather(bf16[32,48,32]{2,0,1:T(8,128)(2,1)S(1)} %copy.51), channel_id=1, replica_groups=mesh['row'=8,'col'=4] {'col'}, dimensions={1}, use_global_device_ids=true | all-gather | bytes 491520 | tf_op jit(solution)/shard_map/all_gather | solution.py:49
  38.1 45.3 %all_gather.19 = bf16[256,48,32]{1,2,0:T(8,128)(2,1)S(1)} all-gather(bf16[32,48,32]{1,2,0:T(8,128)(2,1)S(1)} %fusion.17), channel_id=1, replica_groups=mesh['row'=8,'col'=4] {'row'}, dimensions={0}, use_global_device_ids=true | all-gather | bytes 884736 | tf_op jit(solution)/shard_map/all_gather | solution.py:45
  83.6 3.8 %reshape.108 = bf16[8,2,12288]{2,1,0:T(2,128)(2,1)} reshape(bf16[192,32,32]{2,1,0:T(8,128)(2,1)} %bitcast.89) | data formatting | bytes 786432
  87.4 2.4 copy.56
  89.8 3.6 %all-to-all-start = ((bf16[8,2,12288]{2,1,0:T(2,128)(2,1)}), bf16[8,2,12288]{2,1,0:T(2,128)(2,1)S(1)}, u32[]{:S(2)}, u32[]{:S(2)}) async-start(bf16[8,2,12288]{2,1,0:T(2,128)(2,1)} %reshape.108), calls=%async_computation | async-start | bytes 786432 | tf_op jit(solution)/shard_map/all_to_all | solution.py:53
  93.4 35.2 %all_gather.21 = bf16[256,48]{1,0:T(8,128)(2,1)S(1)} all-gather(bf16[32,48]{1,0:T(8,128)(2,1)S(1)} %get-tuple-element.7), channel_id=1, replica_groups=mesh['row'=8,'col'=4] {'row'}, dimensions={0}, use_global_device_ids=true | all-gather | bytes 27648 | tf_op jit(solution)/shard_map/all_gather | solution.py:46
  131.6 3.7 %convert_bitcast_fusion = bf16[24,48,32,32]{1,2,3,0:T(8,128)(2,1)} fusion(bf16[24,32,256,1]{2,1,3,0:T(8,128)(2,1)S(1)} %bitcast.90, bf16[48,32,256]{2,0,1:T(8,128)(2,1)S(1)} %copy-done.4), kind=kOutput, calls=%fused_computation | convolution fusion | flops 605159424 | bytes 3538944 | tf_op jit(solution)/shard_map/dot_general | solution.py:58
  135.3 17.8 %copy.57 = bf16[24,48,32,32]{3,2,1,0:T(8,128)(2,1)} copy(bf16[24,48,32,32]{1,2,3,0:T(8,128)(2,1)} %convert_bitcast_fusion) | data formatting | bytes 4718592 | tf_op jit(solution)/shard_map/convert_element_type | solution.py:67
  153.1 12.7 %reshape.95 = bf16[24,48,1024]{2,1,0:T(8,128)(2,1)S(1)} reshape(bf16[24,48,32,32]{3,2,1,0:T(8,128)(2,1)} %copy.57) | data formatting | bytes 4718592 | tf_op jit(solution)/shard_map/reshape | solution.py:69
  165.9 1.8 fusion.49
  168.7 1.2 fusion.22
  170.7 48.0 %all-gather.4.cloned.1.call-done = bf16[192,48,128]{2,1,0:T(8,128)(2,1)} async-done(((bf16[24,48,128]{2,1,0:T(8,128)(2,1)}), bf16[192,48,128]{2,1,0:T(8,128)(2,1)}) %all-gather.4.cloned.1.call-update) | async-done | bytes 2359312 | tf_op jit(solution)/shard_map/all_gather | solution.py:92
  218.7 3.9 %all-to-all-start.2 = ((bf16[192,48,128]{2,1,0:T(8,128)(2,1)}), bf16[192,48,128]{2,1,0:T(8,128)(2,1)S(1)}, u32[]{:S(2)}, u32[]{:S(2)}) async-start(bf16[192,48,128]{2,1,0:T(8,128)(2,1)} %all-gather.4.cloned.1.call-done), calls=%async_computation.2 | async-start | bytes 4718592 | tf_op jit(solution)/shard_map/all_to_all | solution.py:93
  222.6 1.3 fusion.9
  223.9 18.8 %all-gather.6.cloned.1.call-done = bf16[24,192,128]{2,1,0:T(8,128)(2,1)} async-done(((bf16[24,48,128]{2,1,0:T(8,128)(2,1)}), bf16[24,192,128]{2,1,0:T(8,128)(2,1)}) %all-gather.6.cloned.1.call-update) | async-done | bytes 1179664 | tf_op jit(solution)/shard_map/all_gather | solution.py:96
  242.7 2.8 %copy.63 = bf16[24,192,128]{1,0,2:T(8,128)(2,1)} copy(bf16[24,192,128]{2,1,0:T(8,128)(2,1)} %all-gather.6.cloned.1.call-done) | data formatting | bytes 2359296 | tf_op jit(solution)/shard_map/all_gather | solution.py:96
  245.5 11.6 %all-to-all-done.2 = bf16[192,48,128]{2,1,0:T(8,128)(2,1)S(1)} async-done(((bf16[192,48,128]{2,1,0:T(8,128)(2,1)}), bf16[192,48,128]{2,1,0:T(8,128)(2,1)S(1)}, u32[]{:S(2)}, u32[]{:S(2)}) %all-to-all-start.2) | async-done | bytes 2359328 | tf_op jit(solution)/shard_map/all_to_all | solution.py:93
  257.1 2.1 copy.61
  259.2 3.8 %copy.62 = bf16[48,192,128]{1,0,2:T(8,128)(2,1)S(1)} copy(bf16[48,192,128]{2,1,0:T(8,128)(2,1)} %bitcast.86) | data formatting | bytes 4718592 | tf_op jit(solution)/shard_map/all_to_all | solution.py:93
  263.0 2.4 bitcast_reduce_fusion
  267.8 1.5 fusion.15
  (69 shorter events, 11.6 us)
Async XLA Ops:
  6.5 159.3 %copy-start = (bf16[1024,128]{1,0:T(8,128)(2,1)S(1)}, bf16[1024,128]{1,0:T(8,128)(2,1)}, u32[]{:S(2)}) copy-start(bf16[1024,128]{1,0:T(8,128)(2,1)} %param.18) | copy-start | bytes 786436
  6.5 15.7 %copy-start.3 = (bf16[32,48,256]{2,1,0:T(8,128)(2,1)S(1)}, bf16[32,48,256]{2,1,0:T(8,128)(2,1)}, u32[]{:S(2)}) copy-start(bf16[32,48,256]{2,1,0:T(8,128)(2,1)} %param.12) | copy-start | bytes 2359300
  6.5 16.2 %copy-start.11 = (bf16[256,32]{0,1:T(8,128)(2,1)S(1)}, bf16[256,32]{0,1:T(8,128)(2,1)}, u32[]{:S(2)}) copy-start(bf16[256,32]{0,1:T(8,128)(2,1)} %param.16) | copy-start | bytes 49156
  14.5 75.3 %all-to-all-start.1 = ((bf16[8,2,384]{2,1,0:T(2,128)(2,1)}), bf16[8,2,384]{2,1,0:T(2,128)(2,1)S(1)}, u32[]{:S(2)}, u32[]{:S(2)}) async-start(bf16[8,2,384]{2,1,0:T(2,128)(2,1)} %reshape.110), calls=%async_computation.1 | async-start | bytes 24576 | tf_op jit(solution)/shard_map/all_to_all | solution.py:54
  23.4 14.0 %copy-start.12 = (bf16[256,32]{0,1:T(8,128)(2,1)S(1)}, bf16[256,32]{0,1:T(8,128)(2,1)}, u32[]{:S(2)}) copy-start(bf16[256,32]{0,1:T(8,128)(2,1)} %param.17) | copy-start | bytes 49156
  38.1 45.4 %copy-start.13 = (s32[192]{0:T(256)S(1)}, s32[192]{0:T(256)}, u32[]{:S(2)}) copy-start(s32[192]{0:T(256)} %param.14) | copy-start | bytes 2308
  89.8 39.2 %all-to-all-start = ((bf16[8,2,12288]{2,1,0:T(2,128)(2,1)}), bf16[8,2,12288]{2,1,0:T(2,128)(2,1)S(1)}, u32[]{:S(2)}, u32[]{:S(2)}) async-start(bf16[8,2,12288]{2,1,0:T(2,128)(2,1)} %reshape.108), calls=%async_computation | async-start | bytes 786432 | tf_op jit(solution)/shard_map/all_to_all | solution.py:53
  93.4 125.3 %all-gather.4.cloned.1.call-start = ((), (), s32[]{:S(2)}) async-start(), calls=%async_computation.3 | async-start | bytes 2654208 | tf_op jit(solution)/shard_map/all_gather | solution.py:92
  130.4 1.2 copy-start.4
  165.9 2.3 copy-start.6
  167.7 54.8 %copy-start.1 = (f32[24,48,128]{2,1,0:T(8,128)}, f32[24,48,128]{2,1,0:T(8,128)S(1)}, u32[]{:S(2)}) copy-start(f32[24,48,128]{2,1,0:T(8,128)S(1)} %get-tuple-element.10) | copy-start | bytes 1769476
  169.9 72.8 %all-gather.6.cloned.1.call-start = ((), (), s32[]{:S(2)}) async-start(), calls=%async_computation.4 | async-start | bytes 1474560 | tf_op jit(solution)/shard_map/all_gather | solution.py:96
  170.7 51.9 %copy-start.10 = (bf16[128,128]{1,0:T(8,128)(2,1)S(1)}, bf16[128,128]{1,0:T(8,128)(2,1)}, u32[]{:S(2)}) copy-start(bf16[128,128]{1,0:T(8,128)(2,1)} %param.20) | copy-start | bytes 98308
  218.7 38.4 %all-to-all-start.2 = ((bf16[192,48,128]{2,1,0:T(8,128)(2,1)}), bf16[192,48,128]{2,1,0:T(8,128)(2,1)S(1)}, u32[]{:S(2)}, u32[]{:S(2)}) async-start(bf16[192,48,128]{2,1,0:T(8,128)(2,1)} %all-gather.4.cloned.1.call-done), calls=%async_computation.2 | async-start | bytes 4718592 | tf_op jit(solution)/shard_map/all_to_all | solution.py:93
  265.6 1.1 copy-start.2
  265.6 1.2 copy-start.5
  265.6 1.2 copy-start.7
  266.9 0.9 copy-start.8
  266.9 1.0 copy-start.9
Sparse Core Ops, SparseCore 0:
  170.0 48.6 all-gather.3
  220.2 22.3 all-gather.5
where the time goes:
time: 277 us; the launch traced here: 276 us
  blocking collectives  100 us (36%)
  waiting for transfers between devices  79.1 us (29%)
  local copies, waits for them, and re-layouts  50.8 us (18%)
  starting transfers between devices  13.7 us (5%)
  between operations  13.7 us (5%)
  matrix products  13.2 us (5%)
  other arithmetic  5.45 us (2%)
    all_gather x1, waiting for transfers between devices, shards(): right_cols = lax.all_gather(right_tri, 'row', axis=0, tiled=True)  48 us
    all_gather x1, blocking collectives, shards(): lax.all_gather(right_side, 'row', axis=0, tiled=True)  45.3 us
    all_gather x1, blocking collectives, shards(): lax.all_gather(mask_wire, 'row', axis=0, tiled=True)  35.2 us
    all_gather x1, waiting for transfers between devices, shards(): lax.all_gather(left_tri, 'col', axis=1, tiled=True)  18.8 us
    convert_element_type x1, local copies, waits for them, and re-layouts, shards(): outer = outer.reshape(block_rows, narrow, block_cols, narrow).transpose(0...  17.8 us
    all_gather x1, blocking collectives, shards(): lax.all_gather(left_side, 'col', axis=1, tiled=True)  13.4 us
    reshape x1, local copies, waits for them, and re-layouts, shards(): outer = outer.reshape(block_rows, block_cols, narrow * narrow)  12.7 us
    all_to_all x1, waiting for transfers between devices, shards(): lax.all_to_all(right_cols, 'col', split_axis=0, concat_axis=1, tiled=True)  11.6 us
  transfers between devices with their start and end apart: 5, of which 3 were waited for; matrix products, arithmetic and copies ran while one was open for 5% of the time, Pallas kernels for 0%

commit v1 on v0

--- a/solution.py
+++ b/solution.py
@@ -4,6 +4,22 @@
 from jax.sharding import PartitionSpec as P
 
 epsilon = 1e-05
+
+
+def summed_both_ways(array, axis, dim, product):
+    size, index, width = (lax.axis_size(axis), lax.axis_index(axis), array.shape[dim])
+    forward = [(i, (i + 1) % size) for i in range(size)]
+    left = [(i, (i - 1) % size) for i in range(size)]
+    half = size // 2
+    from_left = from_right = array
+    subtotal = product(array, index * width)
+    for turn in range(1, half + 1):
+        from_left = lax.ppermute(from_left, axis, forward)
+        if turn < size - half:
+            from_right = lax.ppermute(from_right, axis, left)
+            subtotal = subtotal + product(from_right, (index + turn) % size * width)
+        subtotal = subtotal + product(from_left, (index - turn) % size * width)
+    return subtotal
 
 
 def normalize(values):
@@ -91,11 +107,16 @@
     ).astype(jnp.bfloat16)
     right_cols = lax.all_gather(right_tri, "row", axis=0, tiled=True)
     right_rows = lax.all_to_all(right_cols, "col", split_axis=0, concat_axis=1, tiled=True)
-    summed = jnp.einsum(
-        "ikc,jkc->ijc",
-        lax.all_gather(left_tri, "col", axis=1, tiled=True),
-        right_rows,
-        preferred_element_type=jnp.float32,
+    summed = summed_both_ways(
+        left_tri,
+        "col",
+        1,
+        lambda shard, start: jnp.einsum(
+            "ikc,jkc->ijc",
+            shard,
+            lax.dynamic_slice_in_dim(right_rows, start, shard.shape[1], axis=1),
+            preferred_element_type=jnp.float32,
+        ),
     )
     normed_sum = normalize(summed).astype(jnp.bfloat16)
     update = jax.nn.sigmoid(

time: 277 us -> 293 us (1.058)
  local copies, waits for them, and re-layouts: 50.8 us -> 58.8 us
  matrix products: 13.2 us -> 17.1 us
    ppermute x0 -> x3, waiting for transfers between devices: none -> 32.5 us  [the longest x2 32.5 us: summed_both_ways(): from_left = lax.ppermute(from_left, axis, forward)]
    all_gather x1 -> x0, waiting for transfers between devices: 18.8 us -> none  [shards(): lax.all_gather(left_tri, 'col', axis=1, tiled=True)]
    all_to_all x1, waiting for transfers between devices: 11.6 us -> 0.01 us  [shards(): lax.all_to_all(right_cols, 'col', split_axis=0, concat_axis=1, tiled=True)]
    unnamed x33 -> x43, local copies, waits for them, and re-layouts: 6.54 us -> 13.2 us
    ppermute x0 -> x3, local copies, waits for them, and re-layouts: none -> 6.63 us  [the longest x2 4.42 us: summed_both_ways(): from_left = lax.ppermute(from_left, axis, forward)]
    all_to_all x2 -> x1, local copies, waits for them, and re-layouts: 5.89 us -> 0.71 us  [shards(): lax.all_to_all(right_cols, 'col', split_axis=0, concat_axis=1, tiled=True)]
    dot_general x1 -> x4, matrix products: 2.35 us -> 5.48 us  [shards(): jnp.einsum('ikc,jkc->ijc', shard, lax.dynamic_slice_in_dim(right_rows, st...]
  transfers between devices with their start and end apart: 5 -> 7, of which waited for: 3 -> 2; matrix products, arithmetic and copies ran while one was open for 5% -> 7% of each run, Pallas kernels for 0% -> 0%
where the time goes in v1:
time: 293 us; the launch traced here: 292 us
  blocking collectives  100 us (34%)
  waiting for transfers between devices  81.3 us (28%)
  local copies, waits for them, and re-layouts  58.8 us (20%)
  matrix products  17.1 us (6%)
  starting transfers between devices  15.3 us (5%)
  between operations  13.8 us (5%)
  other arithmetic  5.36 us (2%)
    all_gather x1, waiting for transfers between devices, shards(): right_cols = lax.all_gather(right_tri, 'row', axis=0, tiled=True)  48.8 us
    all_gather x1, blocking collectives, shards(): lax.all_gather(right_side, 'row', axis=0, tiled=True)  45.3 us
    all_gather x1, blocking collectives, shards(): lax.all_gather(mask_wire, 'row', axis=0, tiled=True)  35.2 us
    ppermute x2, waiting for transfers between devices, summed_both_ways(): from_left = lax.ppermute(from_left, axis, forward)  32.5 us
    convert_element_type x1, local copies, waits for them, and re-layouts, shards(): outer = outer.reshape(block_rows, narrow, block_cols, narrow).transpose(0...  17.8 us
    all_gather x1, blocking collectives, shards(): lax.all_gather(left_side, 'col', axis=1, tiled=True)  13.4 us
    unnamed x43, local copies, waits for them, and re-layouts  13.2 us
    reshape x1, local copies, waits for them, and re-layouts, shards(): outer = outer.reshape(block_rows, block_cols, narrow * narrow)  12.7 us
  transfers between devices with their start and end apart: 7, of which 2 were waited for; matrix products, arithmetic and copies ran while one was open for 7% of the time, Pallas kernels for 0%

profile of v1, /device:TPU:0, one launch (start us, length us, event | category | flops | bytes accessed | tf_op | source)
XLA Modules:
  0.0 291.7 jit_solution(12543676203472864745)
XLA Ops:
  7.4 6.2 %all-gather = bf16[4,48,32]{1,2,0:T(8,128)(2,1)S(1)} all-gather(bf16[1,48,32]{1,2,0:T(8,128)(2,1)S(1)} %bitcast.99), channel_id=1, replica_groups=mesh['row'=8,'col'=4] {'col'}, dimensions={0}, use_global_device_ids=true | all-gather | bytes 15360 | tf_op jit(solution)/shard_map/all_gather | solution.py:66
  14.5 6.2 %all-to-all-start.1 = ((bf16[8,2,384]{2,1,0:T(2,128)(2,1)}), bf16[8,2,384]{2,1,0:T(2,128)(2,1)S(1)}, u32[]{:S(2)}, u32[]{:S(2)}) async-start(bf16[8,2,384]{2,1,0:T(2,128)(2,1)} %reshape.110), calls=%async_computation.1 | async-start | bytes 24576 | tf_op jit(solution)/shard_map/all_to_all | solution.py:70
  24.1 13.4 %all_gather.15 = bf16[32,192,32]{2,0,1:T(8,128)(2,1)} all-gather(bf16[32,48,32]{2,0,1:T(8,128)(2,1)S(1)} %copy.72), channel_id=1, replica_groups=mesh['row'=8,'col'=4] {'col'}, dimensions={1}, use_global_device_ids=true | all-gather | bytes 491520 | tf_op jit(solution)/shard_map/all_gather | solution.py:65
  38.1 45.3 %all_gather.16 = bf16[256,48,32]{1,2,0:T(8,128)(2,1)S(1)} all-gather(bf16[32,48,32]{1,2,0:T(8,128)(2,1)S(1)} %fusion.17), channel_id=1, replica_groups=mesh['row'=8,'col'=4] {'row'}, dimensions={0}, use_global_device_ids=true | all-gather | bytes 884736 | tf_op jit(solution)/shard_map/all_gather | solution.py:61
  83.6 3.8 %reshape.108 = bf16[8,2,12288]{2,1,0:T(2,128)(2,1)} reshape(bf16[192,32,32]{2,1,0:T(8,128)(2,1)} %bitcast.95) | data formatting | bytes 786432
  87.4 2.4 copy.77
  89.8 3.6 %all-to-all-start = ((bf16[8,2,12288]{2,1,0:T(2,128)(2,1)}), bf16[8,2,12288]{2,1,0:T(2,128)(2,1)S(1)}, u32[]{:S(2)}, u32[]{:S(2)}) async-start(bf16[8,2,12288]{2,1,0:T(2,128)(2,1)} %reshape.108), calls=%async_computation | async-start | bytes 786432 | tf_op jit(solution)/shard_map/all_to_all | solution.py:69
  93.4 35.2 %all_gather.18 = bf16[256,48]{1,0:T(8,128)(2,1)S(1)} all-gather(bf16[32,48]{1,0:T(8,128)(2,1)S(1)} %get-tuple-element.11), channel_id=1, replica_groups=mesh['row'=8,'col'=4] {'row'}, dimensions={0}, use_global_device_ids=true | all-gather | bytes 27648 | tf_op jit(solution)/shard_map/all_gather | solution.py:62
  131.6 3.7 %convert_bitcast_fusion = bf16[24,48,32,32]{1,2,3,0:T(8,128)(2,1)} fusion(bf16[24,32,256,1]{2,1,3,0:T(8,128)(2,1)S(1)} %bitcast.96, bf16[48,32,256]{2,0,1:T(8,128)(2,1)S(1)} %copy-done.5), kind=kOutput, calls=%fused_computation | convolution fusion | flops 605159424 | bytes 3538944 | tf_op jit(solution)/shard_map/dot_general | solution.py:74
  135.3 17.8 %copy.78 = bf16[24,48,32,32]{3,2,1,0:T(8,128)(2,1)} copy(bf16[24,48,32,32]{1,2,3,0:T(8,128)(2,1)} %convert_bitcast_fusion) | data formatting | bytes 4718592 | tf_op jit(solution)/shard_map/convert_element_type | solution.py:83
  153.1 12.7 %reshape.95 = bf16[24,48,1024]{2,1,0:T(8,128)(2,1)S(1)} reshape(bf16[24,48,32,32]{3,2,1,0:T(8,128)(2,1)} %copy.78) | data formatting | bytes 4718592 | tf_op jit(solution)/shard_map/reshape | solution.py:85
  165.9 1.8 fusion.49
  169.8 48.8 %all-gather.3.cloned.1.call-done = bf16[192,48,128]{2,1,0:T(8,128)(2,1)} async-done(((bf16[24,48,128]{2,1,0:T(8,128)(2,1)}), bf16[192,48,128]{2,1,0:T(8,128)(2,1)}) %all-gather.3.cloned.1.call-update) | async-done | bytes 2359312 | tf_op jit(solution)/shard_map/all_gather | solution.py:108
  218.6 3.6 %all-to-all-start.2 = ((bf16[192,48,128]{2,1,0:T(8,128)(2,1)}), bf16[192,48,128]{2,1,0:T(8,128)(2,1)S(1)}, u32[]{:S(2)}, u32[]{:S(2)}) async-start(bf16[192,48,128]{2,1,0:T(8,128)(2,1)} %all-gather.3.cloned.1.call-done), calls=%async_computation.2 | async-start | bytes 4718592 | tf_op jit(solution)/shard_map/all_to_all | solution.py:109
  224.0 32.5 %collective-permute-done.1 = bf16[24,48,128]{2,1,0:T(8,128)(2,1)} collective-permute-done((bf16[24,48,128]{2,1,0:T(8,128)(2,1)S(1)}, bf16[24,48,128]{2,1,0:T(8,128)(2,1)}, u32[]{:S(2)}, u32[]{:S(2)}) %collective-permute-start.1) | collective-permute-done | bytes 294944 | tf_op jit(solution)/shard_map/ppermute | solution.py:17
  257.8 2.1 fusion.9
  259.9 2.2 copy.88
  262.1 2.2 copy.86
  264.3 2.2 copy.90
  268.6 1.7 copy.98
  270.3 1.8 copy.97
  273.0 1.8 copy.100
  274.9 2.7 fusion.52
  283.3 1.5 fusion.15
  (88 shorter events, 22.6 us)
Async XLA Ops:
  6.5 159.3 %copy-start = (bf16[1024,128]{1,0:T(8,128)(2,1)S(1)}, bf16[1024,128]{1,0:T(8,128)(2,1)}, u32[]{:S(2)}) copy-start(bf16[1024,128]{1,0:T(8,128)(2,1)} %param.18) | copy-start | bytes 786436
  6.5 15.7 %copy-start.4 = (bf16[32,48,256]{2,1,0:T(8,128)(2,1)S(1)}, bf16[32,48,256]{2,1,0:T(8,128)(2,1)}, u32[]{:S(2)}) copy-start(bf16[32,48,256]{2,1,0:T(8,128)(2,1)} %param.12) | copy-start | bytes 2359300
  6.5 16.2 %copy-start.14 = (bf16[256,32]{0,1:T(8,128)(2,1)S(1)}, bf16[256,32]{0,1:T(8,128)(2,1)}, u32[]{:S(2)}) copy-start(bf16[256,32]{0,1:T(8,128)(2,1)} %param.16) | copy-start | bytes 49156
  14.5 75.2 %all-to-all-start.1 = ((bf16[8,2,384]{2,1,0:T(2,128)(2,1)}), bf16[8,2,384]{2,1,0:T(2,128)(2,1)S(1)}, u32[]{:S(2)}, u32[]{:S(2)}) async-start(bf16[8,2,384]{2,1,0:T(2,128)(2,1)} %reshape.110), calls=%async_computation.1 | async-start | bytes 24576 | tf_op jit(solution)/shard_map/all_to_all | solution.py:70
  23.4 14.0 %copy-start.15 = (bf16[256,32]{0,1:T(8,128)(2,1)S(1)}, bf16[256,32]{0,1:T(8,128)(2,1)}, u32[]{:S(2)}) copy-start(bf16[256,32]{0,1:T(8,128)(2,1)} %param.17) | copy-start | bytes 49156
  38.1 45.4 %copy-start.16 = (s32[192]{0:T(256)S(1)}, s32[192]{0:T(256)}, u32[]{:S(2)}) copy-start(s32[192]{0:T(256)} %param.14) | copy-start | bytes 2308
  89.8 39.2 %all-to-all-start = ((bf16[8,2,12288]{2,1,0:T(2,128)(2,1)}), bf16[8,2,12288]{2,1,0:T(2,128)(2,1)S(1)}, u32[]{:S(2)}, u32[]{:S(2)}) async-start(bf16[8,2,12288]{2,1,0:T(2,128)(2,1)} %reshape.108), calls=%async_computation | async-start | bytes 786432 | tf_op jit(solution)/shard_map/all_to_all | solution.py:69
  93.4 125.2 %all-gather.3.cloned.1.call-start = ((), (), s32[]{:S(2)}) async-start(), calls=%async_computation.3 | async-start | bytes 2654208 | tf_op jit(solution)/shard_map/all_gather | solution.py:108
  130.4 1.2 copy-start.5
  165.9 2.3 copy-start.10
  167.7 90.1 %copy-start.2 = (f32[24,48,128]{2,1,0:T(8,128)}, f32[24,48,128]{2,1,0:T(8,128)S(1)}, u32[]{:S(2)}) copy-start(f32[24,48,128]{2,1,0:T(8,128)S(1)} %get-tuple-element.14) | copy-start | bytes 1769476
  218.6 47.9 %all-to-all-start.2 = ((bf16[192,48,128]{2,1,0:T(8,128)(2,1)}), bf16[192,48,128]{2,1,0:T(8,128)(2,1)S(1)}, u32[]{:S(2)}, u32[]{:S(2)}) async-start(bf16[192,48,128]{2,1,0:T(8,128)(2,1)} %all-gather.3.cloned.1.call-done), calls=%async_computation.2 | async-start | bytes 4718592 | tf_op jit(solution)/shard_map/all_to_all | solution.py:109
  222.2 34.3 %collective-permute-start.1 = (bf16[24,48,128]{2,1,0:T(8,128)(2,1)S(1)}, bf16[24,48,128]{2,1,0:T(8,128)(2,1)}, u32[]{:S(2)}, u32[]{:S(2)}) collective-permute-start(bf16[24,48,128]{2,1,0:T(8,128)(2,1)S(1)} %get-tuple-element.5), channel_id=1, source_target_pairs={{0,1},{1,2},{2,3},{3,0},{4,5},{5,6},{6,7},{7,4},{8,9},{9,10},{10,1... | collective-permute-start | bytes 884744 | tf_op jit(solution)/shard_map/ppermute | solution.py:17
  222.7 39.4 %collective-permute-start = (bf16[24,48,128]{2,1,0:T(8,128)(2,1)S(1)}, bf16[24,48,128]{2,1,0:T(8,128)(2,1)}, u32[]{:S(2)}, u32[]{:S(2)}) collective-permute-start(bf16[24,48,128]{2,1,0:T(8,128)(2,1)S(1)} %get-tuple-element.5), channel_id=1, source_target_pairs={{0,3},{1,0},{2,1},{3,2},{4,7},{5,4},{6,5},{7,6},{8,11},{9,8},{10,9... | collective-permute-start | bytes 884744 | tf_op jit(solution)/shard_map/ppermute | solution.py:19
  256.5 7.8 %collective-permute-start.2 = (bf16[24,48,128]{2,1,0:T(8,128)(2,1)}, bf16[24,48,128]{2,1,0:T(8,128)(2,1)}, u32[]{:S(2)}, u32[]{:S(2)}) collective-permute-start(bf16[24,48,128]{2,1,0:T(8,128)(2,1)} %collective-permute-done.1), channel_id=1, source_target_pairs={{0,1},{1,2},{2,3},{3,0},{4,5},{5,6},{6,7},{7,4},{8,9},{9,10},{10,1... | collective-permute-start | bytes 884744 | tf_op jit(solution)/shard_map/ppermute | solution.py:17
  274.9 2.7 copy-start.1
  274.9 2.7 copy-start.7
  277.6 1.1 copy-start.8
  278.7 1.1 copy-start.6
  281.1 1.1 copy-start.3
  281.1 1.2 copy-start.9
  281.1 1.2 copy-start.11
  282.4 0.9 copy-start.12
  282.4 1.0 copy-start.13
Sparse Core Ops, SparseCore 0:
  169.9 48.6 all-gather.2
